TPU v7x, 32 devices: a whole 2x2x4 slice. The times are simulated.
32 devices in a mesh: vec: 16 (over z, y, x), row: 2 (over core).
Axes of the slice: x: 2, y: 2, z: 4, core: 2. Of those that a mesh axis runs over, the one named last changes fastest.
Arguments:
- vectors: bfloat16 [2, 4096, 1024], P('row', 'vec'), may hold values from -6 to 6
- rotation: bfloat16 [1024, 1024], P(None, 'vec'), may hold values from -0.1875 to 0.1875
- blocks: bfloat16 [64, 8, 128, 128], P('row'), may hold values from -0.125 to 0.125
- column_blocks: int32 [64, 8], P('row'), may hold values from -2 to 65, as said below
Outputs:
- filtered: bfloat16 [2, 4096, 1024], P('row', 'vec')
Inputs may be any that keep to these rules, and one draw needn't show every extreme that they name: `column_blocks`: block row r of partition p = r // 32 lists 8 distinct column blocks between p * 32 - 2 and p * 32 + 33; the first block row of every partition lists the lowest of these and the last one the highest; column blocks outside 0 to 63 stand for zeros.
All inputs are finite; a program needn't handle non-finite values.
Results may differ from a plain program's by a relative error of at most 0.006.
Values may be sent and summed in bfloat16 or wider, within the bound.
No kernel may reach another device: no remote copies, remote signals or barrier semaphores. Data moves between devices by JAX's collectives and lax.ppermute only.
A program may use at most 64 MiB of HBM per device.

v0:
```python
import jax
import jax.numpy as jnp
from jax import lax
from jax.sharding import PartitionSpec as P

BS = 128
HB = 2
STEPS = 4
centre = 0.3
half_width = 1.2


def with_halo(block, sides, width):
    for axis, dim in sides:
        count = lax.axis_size(axis)
        forward = [(i, i + 1) for i in range(count - 1)]
        backward = [(target, source) for source, target in forward]
        low = lax.ppermute(
            lax.slice_in_dim(block, block.shape[dim] - width, None, axis=dim), axis, forward
        )
        high = lax.ppermute(lax.slice_in_dim(block, 0, width, axis=dim), axis, backward)
        block = jnp.concatenate([low, block, high], axis=dim)
    return block


def apply_matrix(operand, blocks, offsets):
    extended = with_halo(operand, (("row", 1),), HB * BS)
    stacked = extended.reshape(extended.shape[0], -1, BS)
    picked = stacked[:, offsets]
    product = jnp.einsum("rjab,krjb->kra", blocks, picked, preferred_element_type=jnp.float32)
    return product.reshape(extended.shape[0], -1)


def filter_panel(vec_panel, blocks, offsets):
    previous = vec_panel.astype(jnp.float32)
    current = (apply_matrix(vec_panel, blocks, offsets) - centre * previous) / half_width
    for turn_index in range(STEPS - 1):
        operand = current.astype(jnp.bfloat16)
        following = (
            2.0 * (apply_matrix(operand, blocks, offsets) - centre * current) / half_width
            - previous
        )
        previous = current
        current = following
    return current.astype(jnp.bfloat16)


def local(vectors, rotation, blocks, column_blocks):
    local_rows = vectors[0]
    offsets = column_blocks - (lax.axis_index("row") * column_blocks.shape[0] - HB)
    contract = (((0,), (1,)), ((), ()))
    rotated = lax.dot_general(
        lax.all_gather(rotation, "vec", axis=1, tiled=True),
        local_rows,
        contract,
        preferred_element_type=jnp.float32,
    ).astype(jnp.bfloat16)
    vec_panel = lax.all_to_all(rotated, "vec", split_axis=0, concat_axis=1, tiled=True)
    filtered = filter_panel(vec_panel, blocks, offsets)
    returned = lax.all_to_all(filtered, "vec", split_axis=1, concat_axis=0, tiled=True)
    return jnp.transpose(returned)[None]


def solution(mesh):
    placed = (P("row", "vec", None), P(None, "vec"), P("row", None, None, None), P("row", None))
    return jax.shard_map(
        local, mesh=mesh, in_specs=placed, out_specs=P("row", "vec", None), check_vma=False
    )
```

profile of v0, /device:TPU:0, one launch (start us, length us, event | category | flops | bytes accessed | tf_op | source)
XLA Modules:
  0.0 203.2 jit_solution(18180730329563429137)
XLA Ops:
  6.5 0.0 copy-start
  6.5 0.0 all-gather.2.cloned.1.call-start
  6.5 0.7 all-gather.2.cloned.1.call-update
  7.3 66.0 %all-gather.2.cloned.1.call-done = bf16[1024,1024]{0,1:T(8,128)(2,1)} async-done(((bf16[1024,64]{0,1:T(8,128)(2,1)}), bf16[1024,1024]{0,1:T(8,128)(2,1)}) %all-gather.2.cloned.1.call-update) | async-done | bytes 2097168 | tf_op jit(solution)/shard_map/all_gather | solution.py:53
  73.2 0.0 copy-done
  73.2 3.1 %convolution_convert_fusion = bf16[1024,256]{1,0:T(8,128)(2,1)} fusion(bf16[1024,1024]{0,1:T(8,128)(2,1)} %all-gather.2.cloned.1.call-done, bf16[1,256,1024]{2,1,0:T(8,128)(2,1)S(1)} %copy-done), kind=kOutput, calls=%fused_computation.9 | convolution fusion | flops 537133056 | bytes 3145728 | tf_op jit(solution)/shard_map/dot_general | solution.py:52
  76.4 4.4 %all-to-all-start = ((bf16[16,64,256]{2,1,0:T(8,128)(2,1)}), bf16[16,64,256]{2,1,0:T(8,128)(2,1)S(1)}, u32[]{:S(2)}, u32[]{:S(2)}) async-start(bf16[16,64,256]{2,1,0:T(8,128)(2,1)} %bitcast.1), calls=%async_computation | async-start | bytes 1048576 | tf_op jit(solution)/shard_map/all_to_all | solution.py:58
  80.8 0.0 copy-done.11
  80.8 0.1 copy.22
  80.9 0.1 reshape.53
  81.0 14.0 %all-to-all-done = bf16[16,64,256]{2,1,0:T(8,128)(2,1)S(1)} async-done(((bf16[16,64,256]{2,1,0:T(8,128)(2,1)}), bf16[16,64,256]{2,1,0:T(8,128)(2,1)S(1)}, u32[]{:S(2)}, u32[]{:S(2)}) %all-to-all-start) | async-done | bytes 524320 | tf_op jit(solution)/shard_map/all_to_all | solution.py:58
  95.0 0.0 copy-start.1
  95.0 1.3 collective-permute-start
  96.3 1.3 collective-permute-start.1
  97.7 0.0 collective-permute-done
  97.7 0.0 copy-done.6
  97.7 1.8 collective-permute-done.1
  99.4 0.2 copy_bitcast_fusion.3
  99.6 3.0 %gather_fusion = bf16[256,64,128]{2,1,0:T(8,128)(2,1)} fusion(bf16[64,36,128]{2,0,1:T(8,128)(2,1)S(1)} %copy_bitcast_fusion.3, s32[1024]{0:T(1024)S(1)} %pad_clamp_fusion), kind=kCustom, calls=%fused_computation | custom fusion | bytes 8389632 | tf_op jit(solution)/shard_map/gather | solution.py:29
  102.7 7.6 %fusion.12 = f32[32,64,128,1]{2,1,3,0:T(8,128)S(1)} fusion(bf16[64,32,8,128]{3,0,2,1:T(8,128)(2,1)} %bitcast.117, bf16[32,8,128,128]{3,2,1,0:T(8,128)(2,1)} %param.6), kind=kOutput, calls=%fused_computation.36 | convolution fusion | flops 536870912 | bytes 13631488 | tf_op jit(solution)/shard_map/rjab,krjb->kra/dot_general | solution.py:30
  110.3 0.0 copy-done.1
  110.3 0.2 multiply_convert_fusion
  110.5 2.1 %collective-permute-start.2 = (bf16[64,256]{1,0:T(8,128)(2,1)S(1)}, bf16[64,256]{1,0:T(8,128)(2,1)S(1)}, u32[]{:S(2)}, u32[]{:S(2)}) collective-permute-start(bf16[64,256]{1,0:T(8,128)(2,1)S(1)} %get-tuple-element.9), channel_id=1, source_target_pairs={{0,1},{2,3},{4,5},{6,7},{8,9},{10,11},{12,13},{14,15},{16,17},{18,... | collective-permute-start | bytes 98312 | tf_op jit(solution)/shard_map/ppermute | solution.py:18
  112.5 1.3 collective-permute-start.3
  113.8 0.0 collective-permute-done.2
  113.8 1.8 collective-permute-done.3
  115.6 0.2 copy_bitcast_fusion.2
  115.8 3.0 %gather_fusion.1 = bf16[256,64,128]{2,1,0:T(8,128)(2,1)} fusion(bf16[64,36,128]{2,0,1:T(8,128)(2,1)S(1)} %copy_bitcast_fusion.2, s32[1024]{0:T(1024)S(1)} %pad_clamp_fusion), kind=kCustom, calls=%fused_computation.1 | custom fusion | bytes 8389632 | tf_op jit(solution)/shard_map/gather | solution.py:29
  118.8 7.6 %fusion.13 = f32[32,64,128,1]{2,1,3,0:T(8,128)S(1)} fusion(bf16[64,32,8,128]{3,0,2,1:T(8,128)(2,1)} %bitcast.118, bf16[32,8,128,128]{3,2,1,0:T(8,128)(2,1)} %param.6), kind=kOutput, calls=%fused_computation.37 | convolution fusion | flops 536870912 | bytes 13631488 | tf_op jit(solution)/shard_map/rjab,krjb->kra/dot_general | solution.py:30
  126.5 0.0 copy-done.2
  126.5 0.3 fusion.7
  126.8 2.1 %collective-permute-start.4 = (bf16[64,256]{1,0:T(8,128)(2,1)S(1)}, bf16[64,256]{1,0:T(8,128)(2,1)S(1)}, u32[]{:S(2)}, u32[]{:S(2)}) collective-permute-start(bf16[64,256]{1,0:T(8,128)(2,1)S(1)} %get-tuple-element.7), channel_id=1, source_target_pairs={{0,1},{2,3},{4,5},{6,7},{8,9},{10,11},{12,13},{14,15},{16,17},{18,... | collective-permute-start | bytes 98312 | tf_op jit(solution)/shard_map/ppermute | solution.py:18
  128.9 1.3 collective-permute-start.5
  130.2 0.0 collective-permute-done.4
  130.2 1.8 collective-permute-done.5
  132.0 0.2 copy_bitcast_fusion.1
  132.1 3.0 %gather_fusion.2 = bf16[256,64,128]{2,1,0:T(8,128)(2,1)} fusion(bf16[64,36,128]{2,0,1:T(8,128)(2,1)S(1)} %copy_bitcast_fusion.1, s32[1024]{0:T(1024)S(1)} %pad_clamp_fusion), kind=kCustom, calls=%fused_computation.2 | custom fusion | bytes 8389632 | tf_op jit(solution)/shard_map/gather | solution.py:29
  135.2 7.6 %fusion.14 = f32[32,64,128,1]{2,1,3,0:T(8,128)S(1)} fusion(bf16[64,32,8,128]{3,0,2,1:T(8,128)(2,1)} %bitcast.119, bf16[32,8,128,128]{3,2,1,0:T(8,128)(2,1)} %param.6), kind=kOutput, calls=%fused_computation.38 | convolution fusion | flops 536870912 | bytes 13631488 | tf_op jit(solution)/shard_map/rjab,krjb->kra/dot_general | solution.py:30
  142.8 0.0 copy-done.3
  142.8 0.0 copy-start.4
  142.8 0.5 fusion.4
  143.3 0.5 copy-done.4
  143.8 2.1 %collective-permute-start.6 = (bf16[64,256]{1,0:T(8,128)(2,1)S(1)}, bf16[64,256]{1,0:T(8,128)(2,1)S(1)}, u32[]{:S(2)}, u32[]{:S(2)}) collective-permute-start(bf16[64,256]{1,0:T(8,128)(2,1)S(1)} %get-tuple-element.5), channel_id=1, source_target_pairs={{0,1},{2,3},{4,5},{6,7},{8,9},{10,11},{12,13},{14,15},{16,17},{18,... | collective-permute-start | bytes 98312 | tf_op jit(solution)/shard_map/ppermute | solution.py:18
  145.9 1.5 collective-permute-start.7
  147.4 0.0 copy-done.9
  147.4 1.6 copy.24
  149.0 2.6 %reshape.50 = f32[64,16,256]{2,1,0:T(8,128)} reshape(f32[64,32,128]{2,1,0:T(8,128)} %copy.24) | data formatting | bytes 2097152 | tf_op jit(solution)/shard_map/reshape | solution.py:31
  151.6 1.6 copy.26
  153.2 1.5 reshape.49
  154.7 0.0 copy-done.5
  154.7 1.6 copy.28
  156.3 2.5 %reshape.48 = f32[64,16,256]{2,1,0:T(8,128)} reshape(f32[64,32,128]{2,1,0:T(8,128)} %copy.28) | data formatting | bytes 2097152 | tf_op jit(solution)/shard_map/reshape | solution.py:31
  158.8 0.0 collective-permute-done.6
  158.8 0.0 collective-permute-done.7
  158.9 0.2 copy_bitcast_fusion
  159.0 3.0 %gather_fusion.3 = bf16[256,64,128]{2,1,0:T(8,128)(2,1)} fusion(bf16[64,36,128]{2,0,1:T(8,128)(2,1)S(1)} %copy_bitcast_fusion, s32[1024]{0:T(1024)S(1)} %pad_clamp_fusion), kind=kCustom, calls=%fused_computation.3 | custom fusion | bytes 8389632 | tf_op jit(solution)/shard_map/gather | solution.py:29
  162.1 7.6 %convolution_bitcast_fusion = f32[64,32,128]{2,0,1:T(8,128)S(1)} fusion(bf16[64,32,8,128]{3,0,2,1:T(8,128)(2,1)} %bitcast.116, bf16[32,8,128,128]{3,2,1,0:T(8,128)(2,1)} %param.6), kind=kOutput, calls=%fused_computation.4 | convolution fusion | flops 536870912 | bytes 13631488 | tf_op jit(solution)/shard_map/rjab,krjb->kra/dot_general | solution.py:30
  169.7 1.6 copy.30
  171.3 2.5 %reshape.47 = f32[64,16,256]{2,1,0:T(8,128)} reshape(f32[64,32,128]{2,1,0:T(8,128)} %copy.30) | data formatting | bytes 2097152 | tf_op jit(solution)/shard_map/reshape | solution.py:31
  173.8 0.0 copy-done.7
  173.8 2.4 %subtract_convert_fusion = bf16[64,16,256]{2,1,0:T(8,128)(2,1)S(1)} fusion(f32[64,16,256]{2,1,0:T(8,128)} %reshape.47, f32[64,16,256]{2,1,0:T(8,128)} %reshape.48, f32[64,16,256]{2,1,0:T(8,128)S(1)} %reshape.49, f32[64,16,256]{2,1,0:T(8,128)S(1)} %copy-done.8, bf16[16,64,256]{2,1,0:T(8,128)(2,1)S(1)} %copy-done.7), kind=kLoop, calls=%fused_computation.18 | loop fusion | flops 4456448 | bytes 5242880 | tf_op jit(solution)/shard_map/convert_element_type | solution.py:45
  176.2 0.2 copy.34
  176.3 19.0 %all_to_all.35 = bf16[64,16,256]{2,0,1:T(8,128)(2,1)S(1)} all-to-all(bf16[64,16,256]{2,0,1:T(8,128)(2,1)S(1)} %copy.34), channel_id=1, replica_groups=mesh['vec'=16,'row'=2] {'vec'}, dimensions={1} | all-to-all | bytes 1048576 | tf_op jit(solution)/shard_map/all_to_all | solution.py:60
  195.3 1.0 copy.35
  (18 shorter events, 0.1 us)
Async XLA Ops:
  6.5 66.7 %copy-start = (bf16[1,256,1024]{2,1,0:T(8,128)(2,1)S(1)}, bf16[1,256,1024]{2,1,0:T(8,128)(2,1)}, u32[]{:S(2)}) copy-start(bf16[1,256,1024]{2,1,0:T(8,128)(2,1)} %param.4) | copy-start | bytes 1572868
  6.5 74.3 %copy-start.11 = (s32[32,8]{0,1:T(8,128)S(1)}, s32[32,8]{0,1:T(8,128)}, u32[]{:S(2)}) copy-start(s32[32,8]{0,1:T(8,128)} %param.7) | copy-start | bytes 3076
  6.5 66.7 %all-gather.2.cloned.1.call-start = ((), (), s32[]{:S(2)}) async-start(), calls=%async_computation.2 | async-start | bytes 2228224 | tf_op jit(solution)/shard_map/all_gather | solution.py:53
  76.4 18.6 %all-to-all-start = ((bf16[16,64,256]{2,1,0:T(8,128)(2,1)}), bf16[16,64,256]{2,1,0:T(8,128)(2,1)S(1)}, u32[]{:S(2)}, u32[]{:S(2)}) async-start(bf16[16,64,256]{2,1,0:T(8,128)(2,1)} %bitcast.1), calls=%async_computation | async-start | bytes 1048576 | tf_op jit(solution)/shard_map/all_to_all | solution.py:58
  95.0 2.7 %copy-start.6 = (bf16[16,64,256]{2,1,0:T(8,128)(2,1)}, bf16[16,64,256]{2,1,0:T(8,128)(2,1)S(1)}, u32[]{:S(2)}) copy-start(bf16[16,64,256]{2,1,0:T(8,128)(2,1)S(1)} %all-to-all-done) | copy-start | bytes 1572868
  95.0 15.2 %copy-start.1 = (bf16[8,8,16,256]{3,1,2,0:T(8,128)(2,1)}, bf16[8,8,16,256]{3,1,2,0:T(8,128)(2,1)S(1)}, u32[]{:S(2)}) copy-start(bf16[8,8,16,256]{3,1,2,0:T(8,128)(2,1)S(1)} %copy.47) | copy-start | bytes 1572868
  95.0 2.6 %collective-permute-start = (bf16[64,256]{1,0:T(8,128)(2,1)S(1)}, bf16[64,256]{1,0:T(8,128)(2,1)S(1)}, u32[]{:S(2)}, u32[]{:S(2)}) collective-permute-start(bf16[64,256]{1,0:T(8,128)(2,1)S(1)} %get-tuple-element.11), channel_id=1, source_target_pairs={{0,1},{2,3},{4,5},{6,7},{8,9},{10,11},{12,13},{14,15},{16,17},{18,... | collective-permute-start | bytes 98312 | tf_op jit(solution)/shard_map/ppermute | solution.py:18
  96.3 3.1 %collective-permute-start.1 = (bf16[64,256]{1,0:T(8,128)(2,1)S(1)}, bf16[64,256]{1,0:T(8,128)(2,1)S(1)}, u32[]{:S(2)}, u32[]{:S(2)}) collective-permute-start(bf16[64,256]{1,0:T(8,128)(2,1)S(1)} %get-tuple-element.12), channel_id=1, source_target_pairs={{1,0},{3,2},{5,4},{7,6},{9,8},{11,10},{13,12},{15,14},{17,16},{19,... | collective-permute-start | bytes 98312 | tf_op jit(solution)/shard_map/ppermute | solution.py:21
  110.5 3.4 %collective-permute-start.2 = (bf16[64,256]{1,0:T(8,128)(2,1)S(1)}, bf16[64,256]{1,0:T(8,128)(2,1)S(1)}, u32[]{:S(2)}, u32[]{:S(2)}) collective-permute-start(bf16[64,256]{1,0:T(8,128)(2,1)S(1)} %get-tuple-element.9), channel_id=1, source_target_pairs={{0,1},{2,3},{4,5},{6,7},{8,9},{10,11},{12,13},{14,15},{16,17},{18,... | collective-permute-start | bytes 98312 | tf_op jit(solution)/shard_map/ppermute | solution.py:18
  112.5 3.1 %collective-permute-start.3 = (bf16[64,256]{1,0:T(8,128)(2,1)S(1)}, bf16[64,256]{1,0:T(8,128)(2,1)S(1)}, u32[]{:S(2)}, u32[]{:S(2)}) collective-permute-start(bf16[64,256]{1,0:T(8,128)(2,1)S(1)} %get-tuple-element.10), channel_id=1, source_target_pairs={{1,0},{3,2},{5,4},{7,6},{9,8},{11,10},{13,12},{15,14},{17,16},{19,... | collective-permute-start | bytes 98312 | tf_op jit(solution)/shard_map/ppermute | solution.py:21
  118.8 7.7 %copy-start.2 = (bf16[8,8,16,256]{3,1,2,0:T(8,128)(2,1)S(1)}, bf16[8,8,16,256]{3,1,2,0:T(8,128)(2,1)}, u32[]{:S(2)}) copy-start(bf16[8,8,16,256]{3,1,2,0:T(8,128)(2,1)} %copy-done.1) | copy-start | bytes 1572868
  126.8 3.4 %collective-permute-start.4 = (bf16[64,256]{1,0:T(8,128)(2,1)S(1)}, bf16[64,256]{1,0:T(8,128)(2,1)S(1)}, u32[]{:S(2)}, u32[]{:S(2)}) collective-permute-start(bf16[64,256]{1,0:T(8,128)(2,1)S(1)} %get-tuple-element.7), channel_id=1, source_target_pairs={{0,1},{2,3},{4,5},{6,7},{8,9},{10,11},{12,13},{14,15},{16,17},{18,... | collective-permute-start | bytes 98312 | tf_op jit(solution)/shard_map/ppermute | solution.py:18
  128.9 3.1 %collective-permute-start.5 = (bf16[64,256]{1,0:T(8,128)(2,1)S(1)}, bf16[64,256]{1,0:T(8,128)(2,1)S(1)}, u32[]{:S(2)}, u32[]{:S(2)}) collective-permute-start(bf16[64,256]{1,0:T(8,128)(2,1)S(1)} %get-tuple-element.8), channel_id=1, source_target_pairs={{1,0},{3,2},{5,4},{7,6},{9,8},{11,10},{13,12},{15,14},{17,16},{19,... | collective-permute-start | bytes 98312 | tf_op jit(solution)/shard_map/ppermute | solution.py:21
  135.2 7.7 %copy-start.3 = (bf16[8,8,16,256]{3,1,2,0:T(8,128)(2,1)S(1)}, bf16[8,8,16,256]{3,1,2,0:T(8,128)(2,1)}, u32[]{:S(2)}) copy-start(bf16[8,8,16,256]{3,1,2,0:T(8,128)(2,1)} %copy-done.1) | copy-start | bytes 1572868
  142.8 1.0 copy-start.4
  143.8 3.6 %copy-start.9 = (bf16[64,4096]{1,0:T(8,128)(2,1)}, bf16[64,4096]{1,0:T(8,128)(2,1)S(1)}, u32[]{:S(2)}) copy-start(bf16[64,4096]{1,0:T(8,128)(2,1)S(1)} %fusion.4) | copy-start | bytes 1572868
  143.8 15.0 %collective-permute-start.6 = (bf16[64,256]{1,0:T(8,128)(2,1)S(1)}, bf16[64,256]{1,0:T(8,128)(2,1)S(1)}, u32[]{:S(2)}, u32[]{:S(2)}) collective-permute-start(bf16[64,256]{1,0:T(8,128)(2,1)S(1)} %get-tuple-element.5), channel_id=1, source_target_pairs={{0,1},{2,3},{4,5},{6,7},{8,9},{10,11},{12,13},{14,15},{16,17},{18,... | collective-permute-start | bytes 98312 | tf_op jit(solution)/shard_map/ppermute | solution.py:18
  145.9 12.9 %collective-permute-start.7 = (bf16[64,256]{1,0:T(8,128)(2,1)S(1)}, bf16[64,256]{1,0:T(8,128)(2,1)S(1)}, u32[]{:S(2)}, u32[]{:S(2)}) collective-permute-start(bf16[64,256]{1,0:T(8,128)(2,1)S(1)} %get-tuple-element.6), channel_id=1, source_target_pairs={{1,0},{3,2},{5,4},{7,6},{9,8},{11,10},{13,12},{15,14},{17,16},{19,... | collective-permute-start | bytes 98312 | tf_op jit(solution)/shard_map/ppermute | solution.py:21
  149.0 5.7 %copy-start.5 = (f32[32,64,128,1]{2,1,3,0:T(8,128)S(1)}, f32[32,64,128,1]{2,1,3,0:T(8,128)}, u32[]{:S(2)}) copy-start(f32[32,64,128,1]{2,1,3,0:T(8,128)} %copy-done.4) | copy-start | bytes 3145732
  151.6 7.2 %copy-start.10 = (bf16[64,4096]{1,0:T(8,128)(2,1)S(1)}, bf16[64,4096]{1,0:T(8,128)(2,1)}, u32[]{:S(2)}) copy-start(bf16[64,4096]{1,0:T(8,128)(2,1)} %copy-done.9) | copy-start | bytes 1572868
  169.7 4.1 %copy-start.7 = (bf16[16,64,256]{2,1,0:T(8,128)(2,1)S(1)}, bf16[16,64,256]{2,1,0:T(8,128)(2,1)}, u32[]{:S(2)}) copy-start(bf16[16,64,256]{2,1,0:T(8,128)(2,1)} %copy-done.6) | copy-start | bytes 1572868
  169.7 4.1 %copy-start.8 = (f32[64,16,256]{2,1,0:T(8,128)S(1)}, f32[64,16,256]{2,1,0:T(8,128)}, u32[]{:S(2)}) copy-start(f32[64,16,256]{2,1,0:T(8,128)} %reshape.50) | copy-start | bytes 3145732
Sparse Core Ops, SparseCore 0:
  10.1 63.0 all-gather.1
where the time goes:
time: 204 us; the launch traced here: 203 us
  waiting for transfers between devices  86 us (42%)
  matrix products  33.6 us (16%)
  local copies, waits for them, and re-layouts  29.7 us (15%)
  blocking collectives  19 us (9%)
  starting transfers between devices  17.3 us (8%)
  between operations  13.7 us (7%)
  other arithmetic  3.9 us (2%)
    all_gather x1, waiting for transfers between devices, local(): lax.all_gather(rotation, 'vec', axis=1, tiled=True)  66 us
    dot_general x4, matrix products, apply_matrix(): jnp.einsum('rjab,krjb->kra', blocks, picked, preferred_element_type=jnp.f...  30.5 us
    all_to_all x1, blocking collectives, local(): lax.all_to_all(filtered, 'vec', split_axis=1, concat_axis=0, tiled=True)  19 us
    all_to_all x1, waiting for transfers between devices, local(): lax.all_to_all(rotated, 'vec', split_axis=0, concat_axis=1, tiled=True)  14 us
    gather x4, local copies, waits for them, and re-layouts, apply_matrix(): picked = stacked[:, offsets]  12.2 us
    reshape x4, local copies, waits for them, and re-layouts, apply_matrix(): return product.reshape(extended.shape[0], -1)  9.18 us
    ppermute x4, starting transfers between devices, with_halo(): lax.ppermute(lax.slice_in_dim(block, block.shape[dim] - width, None, axis...  7.49 us
    transpose x4, local copies, waits for them, and re-layouts, apply_matrix(): jnp.einsum('rjab,krjb->kra', blocks, picked, preferred_element_type=jnp.f...  6.33 us
  transfers between devices with their start and end apart: 10, of which 5 were waited for; matrix products, arithmetic and copies ran while one was open for 6% of the time, Pallas kernels for 0%

commit v1 on v0

--- a/solution.py
+++ b/solution.py
@@ -57,7 +57,10 @@
     ).astype(jnp.bfloat16)
     vec_panel = lax.all_to_all(rotated, "vec", split_axis=0, concat_axis=1, tiled=True)
     filtered = filter_panel(vec_panel, blocks, offsets)
-    returned = lax.all_to_all(filtered, "vec", split_axis=1, concat_axis=0, tiled=True)
+    returned = jnp.concatenate(
+        lax.all_to_all(jnp.stack(jnp.split(filtered, lax.axis_size("vec"), axis=1)), "vec", 0, 0),
+        axis=0,
+    )
     return jnp.transpose(returned)[None]
 
 

time: 204 us -> 188 us (0.922)
  local copies, waits for them, and re-layouts: 29.7 us -> 13.5 us
    reshape x4 -> x0, local copies, waits for them, and re-layouts: 9.18 us -> none  [apply_matrix(): return product.reshape(extended.shape[0], -1)]
    transpose x4 -> x0, local copies, waits for them, and re-layouts: 6.33 us -> none  [apply_matrix(): jnp.einsum('rjab,krjb->kra', blocks, picked, preferred_element_type=jnp.f...]
  transfers between devices with their start and end apart: 10 -> 10, of which waited for: 5 -> 6; matrix products, arithmetic and copies ran while one was open for 6% -> 0% of each run, Pallas kernels for 0% -> 0%
where the time goes in v1:
time: 188 us; the launch traced here: 187 us
  waiting for transfers between devices  87.6 us (47%)
  matrix products  33.7 us (18%)
  blocking collectives  19.1 us (10%)
  starting transfers between devices  17.3 us (9%)
  between operations  13.8 us (7%)
  local copies, waits for them, and re-layouts  13.5 us (7%)
  other arithmetic  2.12 us (1%)
    all_gather x1, waiting for transfers between devices, local(): lax.all_gather(rotation, 'vec', axis=1, tiled=True)  66 us
    dot_general x4, matrix products, apply_matrix(): jnp.einsum('rjab,krjb->kra', blocks, picked, preferred_element_type=jnp.f...  30.6 us
    all_to_all x1, blocking collectives, local(): lax.all_to_all(jnp.stack(jnp.split(filtered, lax.axis_size('vec'), axis=1...  19.1 us
    all_to_all x1, waiting for transfers between devices, local(): lax.all_to_all(rotated, 'vec', split_axis=0, concat_axis=1, tiled=True)  14 us
    gather x4, local copies, waits for them, and re-layouts, apply_matrix(): picked = stacked[:, offsets]  12.1 us
    ppermute x4, starting transfers between devices, with_halo(): lax.ppermute(lax.slice_in_dim(block, block.shape[dim] - width, None, axis...  7.5 us
    ppermute x4, waiting for transfers between devices, with_halo(): lax.ppermute(lax.slice_in_dim(block, 0, width, axis=dim), axis, backward)  6.95 us
    ppermute x4, starting transfers between devices, with_halo(): lax.ppermute(lax.slice_in_dim(block, 0, width, axis=dim), axis, backward)  5.35 us
  transfers between devices with their start and end apart: 10, of which 6 were waited for; matrix products, arithmetic and copies ran while one was open for 0% of the time, Pallas kernels for 0%

profile of v1, /device:TPU:0, one launch (start us, length us, event | category | flops | bytes accessed | tf_op | source)
XLA Modules:
  0.0 187.1 jit_solution(857645403118411049)
XLA Ops:
  6.5 0.0 copy-start
  6.5 0.0 copy-start.6
  6.5 0.0 all-gather.2.cloned.1.call-start
  6.5 0.7 all-gather.2.cloned.1.call-update
  7.3 66.0 %all-gather.2.cloned.1.call-done = bf16[1024,1024]{0,1:T(8,128)(2,1)} async-done(((bf16[1024,64]{0,1:T(8,128)(2,1)}), bf16[1024,1024]{0,1:T(8,128)(2,1)}) %all-gather.2.cloned.1.call-update) | async-done | bytes 2097168 | tf_op jit(solution)/shard_map/all_gather | solution.py:53
  73.2 0.0 copy-done
  73.2 3.1 %convolution_convert_fusion = bf16[1024,256]{1,0:T(8,128)(2,1)} fusion(bf16[1024,1024]{0,1:T(8,128)(2,1)} %all-gather.2.cloned.1.call-done, bf16[1,256,1024]{2,1,0:T(8,128)(2,1)S(1)} %copy-done), kind=kOutput, calls=%fused_computation.10 | convolution fusion | flops 537133056 | bytes 3145728 | tf_op jit(solution)/shard_map/dot_general | solution.py:52
  76.4 4.4 %all-to-all-start = ((bf16[16,64,256]{2,1,0:T(8,128)(2,1)}), bf16[16,64,256]{2,1,0:T(8,128)(2,1)S(1)}, u32[]{:S(2)}, u32[]{:S(2)}) async-start(bf16[16,64,256]{2,1,0:T(8,128)(2,1)} %bitcast.1), calls=%async_computation | async-start | bytes 1048576 | tf_op jit(solution)/shard_map/all_to_all | solution.py:58
  80.8 0.0 copy-done.6
  80.8 0.1 copy.39
  80.9 0.1 reshape.41
  81.0 14.0 %all-to-all-done = bf16[16,64,256]{2,1,0:T(8,128)(2,1)S(1)} async-done(((bf16[16,64,256]{2,1,0:T(8,128)(2,1)}), bf16[16,64,256]{2,1,0:T(8,128)(2,1)S(1)}, u32[]{:S(2)}, u32[]{:S(2)}) %all-to-all-start) | async-done | bytes 524320 | tf_op jit(solution)/shard_map/all_to_all | solution.py:58
  95.0 1.3 collective-permute-start
  96.3 1.3 collective-permute-start.1
  97.6 0.0 collective-permute-done
  97.7 1.8 collective-permute-done.1
  99.4 0.2 copy_bitcast_fusion.3
  99.6 3.0 %gather_fusion = bf16[256,64,128]{2,1,0:T(8,128)(2,1)} fusion(bf16[64,36,128]{2,0,1:T(8,128)(2,1)S(1)} %copy_bitcast_fusion.3, s32[1024]{0:T(1024)S(1)} %pad_clamp_fusion), kind=kCustom, calls=%fused_computation | custom fusion | bytes 8389632 | tf_op jit(solution)/shard_map/gather | solution.py:29
  102.6 7.6 %convolution_bitcast_fusion.3 = f32[32,8,8,128]{3,2,1,0:T(8,128)S(1)} fusion(bf16[64,32,8,128]{3,0,2,1:T(8,128)(2,1)} %bitcast.196, bf16[32,8,128,128]{3,2,1,0:T(8,128)(2,1)} %param.6), kind=kOutput, calls=%fused_computation.7 | convolution fusion | flops 536870912 | bytes 13631488 | tf_op jit(solution)/shard_map/rjab,krjb->kra/dot_general | solution.py:30
  110.2 0.2 multiply_convert_fusion
  110.4 2.1 %collective-permute-start.2 = (bf16[64,256]{1,0:T(8,128)(2,1)S(1)}, bf16[64,256]{1,0:T(8,128)(2,1)S(1)}, u32[]{:S(2)}, u32[]{:S(2)}) collective-permute-start(bf16[64,256]{1,0:T(8,128)(2,1)S(1)} %get-tuple-element.9), channel_id=1, source_target_pairs={{0,1},{2,3},{4,5},{6,7},{8,9},{10,11},{12,13},{14,15},{16,17},{18,... | collective-permute-start | bytes 98312 | tf_op jit(solution)/shard_map/ppermute | solution.py:18
  112.5 1.3 collective-permute-start.3
  113.8 0.0 collective-permute-done.2
  113.8 1.8 collective-permute-done.3
  115.6 0.2 copy_bitcast_fusion.2
  115.8 3.0 %gather_fusion.1 = bf16[256,64,128]{2,1,0:T(8,128)(2,1)} fusion(bf16[64,36,128]{2,0,1:T(8,128)(2,1)S(1)} %copy_bitcast_fusion.2, s32[1024]{0:T(1024)S(1)} %pad_clamp_fusion), kind=kCustom, calls=%fused_computation.1 | custom fusion | bytes 8389632 | tf_op jit(solution)/shard_map/gather | solution.py:29
  118.8 7.6 %convolution_bitcast_fusion.2 = f32[32,8,8,128]{3,2,1,0:T(8,128)S(1)} fusion(bf16[64,32,8,128]{3,0,2,1:T(8,128)(2,1)} %bitcast.197, bf16[32,8,128,128]{3,2,1,0:T(8,128)(2,1)} %param.6), kind=kOutput, calls=%fused_computation.6 | convolution fusion | flops 536870912 | bytes 13631488 | tf_op jit(solution)/shard_map/rjab,krjb->kra/dot_general | solution.py:30
  126.4 0.0 copy-start.1
  126.4 0.3 fusion.25
  126.7 2.1 %collective-permute-start.4 = (bf16[64,256]{1,0:T(8,128)(2,1)S(1)}, bf16[64,256]{1,0:T(8,128)(2,1)S(1)}, u32[]{:S(2)}, u32[]{:S(2)}) collective-permute-start(bf16[64,256]{1,0:T(8,128)(2,1)S(1)} %get-tuple-element.7), channel_id=1, source_target_pairs={{0,1},{2,3},{4,5},{6,7},{8,9},{10,11},{12,13},{14,15},{16,17},{18,... | collective-permute-start | bytes 98312 | tf_op jit(solution)/shard_map/ppermute | solution.py:18
  128.8 1.3 collective-permute-start.5
  130.1 0.0 collective-permute-done.4
  130.1 0.0 copy-done.1
  130.1 1.8 collective-permute-done.5
  131.9 0.2 copy_bitcast_fusion.1
  132.0 3.0 %gather_fusion.2 = bf16[256,64,128]{2,1,0:T(8,128)(2,1)} fusion(bf16[64,36,128]{2,0,1:T(8,128)(2,1)S(1)} %copy_bitcast_fusion.1, s32[1024]{0:T(1024)S(1)} %pad_clamp_fusion), kind=kCustom, calls=%fused_computation.2 | custom fusion | bytes 8389632 | tf_op jit(solution)/shard_map/gather | solution.py:29
  135.1 0.0 copy-start.2
  135.1 7.7 %convolution_bitcast_fusion.1 = f32[32,8,8,128]{3,2,1,0:T(8,128)S(1)} fusion(bf16[64,32,8,128]{3,0,2,1:T(8,128)(2,1)} %bitcast.198, bf16[32,8,128,128]{3,2,1,0:T(8,128)(2,1)} %param.6), kind=kOutput, calls=%fused_computation.5 | convolution fusion | flops 536870912 | bytes 13631488 | tf_op jit(solution)/shard_map/rjab,krjb->kra/dot_general | solution.py:30
  142.7 0.0 copy-done.2
  142.8 0.0 copy-start.4
  142.8 0.5 fusion.24
  143.2 2.1 %collective-permute-start.6 = (bf16[64,256]{1,0:T(8,128)(2,1)S(1)}, bf16[64,256]{1,0:T(8,128)(2,1)S(1)}, u32[]{:S(2)}, u32[]{:S(2)}) collective-permute-start(bf16[64,256]{1,0:T(8,128)(2,1)S(1)} %get-tuple-element.5), channel_id=1, source_target_pairs={{0,1},{2,3},{4,5},{6,7},{8,9},{10,11},{12,13},{14,15},{16,17},{18,... | collective-permute-start | bytes 98312 | tf_op jit(solution)/shard_map/ppermute | solution.py:18
  145.3 1.5 collective-permute-start.7
  146.8 0.0 collective-permute-done.6
  146.8 0.0 copy-done.4
  146.8 1.6 collective-permute-done.7
  148.4 0.2 copy_bitcast_fusion
  148.6 3.0 %gather_fusion.3 = bf16[256,64,128]{2,1,0:T(8,128)(2,1)} fusion(bf16[64,36,128]{2,0,1:T(8,128)(2,1)S(1)} %copy_bitcast_fusion, s32[1024]{0:T(1024)S(1)} %pad_clamp_fusion), kind=kCustom, calls=%fused_computation.3 | custom fusion | bytes 8389632 | tf_op jit(solution)/shard_map/gather | solution.py:29
  151.6 0.0 copy-start.3
  151.6 0.0 copy-start.5
  151.6 7.7 %convolution_bitcast_fusion = f32[32,8,8,128]{3,2,1,0:T(8,128)S(1)} fusion(bf16[64,32,8,128]{3,0,2,1:T(8,128)(2,1)} %bitcast.195, bf16[32,8,128,128]{3,2,1,0:T(8,128)(2,1)} %param.6), kind=kOutput, calls=%fused_computation.4 | convolution fusion | flops 536870912 | bytes 13631488 | tf_op jit(solution)/shard_map/rjab,krjb->kra/dot_general | solution.py:30
  159.4 0.0 copy-done.3
  159.4 0.0 copy-done.5
  159.4 0.6 fusion.3
  160.2 19.1 %all_to_all.24 = bf16[16,64,256]{2,1,0:T(8,128)(2,1)S(1)} all-to-all(bf16[16,64,256]{2,1,0:T(8,128)(2,1)S(1)} %fusion.8), channel_id=1, replica_groups=mesh['vec'=16,'row'=2] {'vec'}, dimensions={0} | all-to-all | bytes 1048576 | tf_op jit(solution)/shard_map/all_to_all | solution.py:61
  179.3 1.0 copy.48
  (23 shorter events, 0.2 us)
Async XLA Ops:
  6.5 66.7 %copy-start = (bf16[1,256,1024]{2,1,0:T(8,128)(2,1)S(1)}, bf16[1,256,1024]{2,1,0:T(8,128)(2,1)}, u32[]{:S(2)}) copy-start(bf16[1,256,1024]{2,1,0:T(8,128)(2,1)} %param.4) | copy-start | bytes 1572868
  6.5 74.3 %copy-start.6 = (s32[32,8]{0,1:T(8,128)S(1)}, s32[32,8]{0,1:T(8,128)}, u32[]{:S(2)}) copy-start(s32[32,8]{0,1:T(8,128)} %param.7) | copy-start | bytes 3076
  6.5 66.7 %all-gather.2.cloned.1.call-start = ((), (), s32[]{:S(2)}) async-start(), calls=%async_computation.2 | async-start | bytes 2228224 | tf_op jit(solution)/shard_map/all_gather | solution.py:53
  76.4 18.6 %all-to-all-start = ((bf16[16,64,256]{2,1,0:T(8,128)(2,1)}), bf16[16,64,256]{2,1,0:T(8,128)(2,1)S(1)}, u32[]{:S(2)}, u32[]{:S(2)}) async-start(bf16[16,64,256]{2,1,0:T(8,128)(2,1)} %bitcast.1), calls=%async_computation | async-start | bytes 1048576 | tf_op jit(solution)/shard_map/all_to_all | solution.py:58
  95.0 2.6 %collective-permute-start = (bf16[64,256]{1,0:T(8,128)(2,1)S(1)}, bf16[64,256]{1,0:T(8,128)(2,1)S(1)}, u32[]{:S(2)}, u32[]{:S(2)}) collective-permute-start(bf16[64,256]{1,0:T(8,128)(2,1)S(1)} %get-tuple-element.11), channel_id=1, source_target_pairs={{0,1},{2,3},{4,5},{6,7},{8,9},{10,11},{12,13},{14,15},{16,17},{18,... | collective-permute-start | bytes 98312 | tf_op jit(solution)/shard_map/ppermute | solution.py:18
  96.3 3.1 %collective-permute-start.1 = (bf16[64,256]{1,0:T(8,128)(2,1)S(1)}, bf16[64,256]{1,0:T(8,128)(2,1)S(1)}, u32[]{:S(2)}, u32[]{:S(2)}) collective-permute-start(bf16[64,256]{1,0:T(8,128)(2,1)S(1)} %get-tuple-element.12), channel_id=1, source_target_pairs={{1,0},{3,2},{5,4},{7,6},{9,8},{11,10},{13,12},{15,14},{17,16},{19,... | collective-permute-start | bytes 98312 | tf_op jit(solution)/shard_map/ppermute | solution.py:21
  110.4 3.4 %collective-permute-start.2 = (bf16[64,256]{1,0:T(8,128)(2,1)S(1)}, bf16[64,256]{1,0:T(8,128)(2,1)S(1)}, u32[]{:S(2)}, u32[]{:S(2)}) collective-permute-start(bf16[64,256]{1,0:T(8,128)(2,1)S(1)} %get-tuple-element.9), channel_id=1, source_target_pairs={{0,1},{2,3},{4,5},{6,7},{8,9},{10,11},{12,13},{14,15},{16,17},{18,... | collective-permute-start | bytes 98312 | tf_op jit(solution)/shard_map/ppermute | solution.py:18
  112.5 3.1 %collective-permute-start.3 = (bf16[64,256]{1,0:T(8,128)(2,1)S(1)}, bf16[64,256]{1,0:T(8,128)(2,1)S(1)}, u32[]{:S(2)}, u32[]{:S(2)}) collective-permute-start(bf16[64,256]{1,0:T(8,128)(2,1)S(1)} %get-tuple-element.10), channel_id=1, source_target_pairs={{1,0},{3,2},{5,4},{7,6},{9,8},{11,10},{13,12},{15,14},{17,16},{19,... | collective-permute-start | bytes 98312 | tf_op jit(solution)/shard_map/ppermute | solution.py:21
  126.4 3.7 %copy-start.1 = (f32[32,8,8,128]{3,2,1,0:T(8,128)}, f32[32,8,8,128]{3,2,1,0:T(8,128)S(1)}, u32[]{:S(2)}) copy-start(f32[32,8,8,128]{3,2,1,0:T(8,128)S(1)} %convolution_bitcast_fusion.2) | copy-start | bytes 3145732
  126.7 3.4 %collective-permute-start.4 = (bf16[64,256]{1,0:T(8,128)(2,1)S(1)}, bf16[64,256]{1,0:T(8,128)(2,1)S(1)}, u32[]{:S(2)}, u32[]{:S(2)}) collective-permute-start(bf16[64,256]{1,0:T(8,128)(2,1)S(1)} %get-tuple-element.7), channel_id=1, source_target_pairs={{0,1},{2,3},{4,5},{6,7},{8,9},{10,11},{12,13},{14,15},{16,17},{18,... | collective-permute-start | bytes 98312 | tf_op jit(solution)/shard_map/ppermute | solution.py:18
  128.8 3.1 %collective-permute-start.5 = (bf16[64,256]{1,0:T(8,128)(2,1)S(1)}, bf16[64,256]{1,0:T(8,128)(2,1)S(1)}, u32[]{:S(2)}, u32[]{:S(2)}) collective-permute-start(bf16[64,256]{1,0:T(8,128)(2,1)S(1)} %get-tuple-element.8), channel_id=1, source_target_pairs={{1,0},{3,2},{5,4},{7,6},{9,8},{11,10},{13,12},{15,14},{17,16},{19,... | collective-permute-start | bytes 98312 | tf_op jit(solution)/shard_map/ppermute | solution.py:21
  135.1 7.7 %copy-start.2 = (f32[32,8,8,128]{3,2,1,0:T(8,128)S(1)}, f32[32,8,8,128]{3,2,1,0:T(8,128)}, u32[]{:S(2)}) copy-start(f32[32,8,8,128]{3,2,1,0:T(8,128)} %copy-done.1) | copy-start | bytes 3145732
  142.8 4.1 %copy-start.4 = (f32[32,8,8,128]{3,2,1,0:T(8,128)}, f32[32,8,8,128]{3,2,1,0:T(8,128)S(1)}, u32[]{:S(2)}) copy-start(f32[32,8,8,128]{3,2,1,0:T(8,128)S(1)} %convolution_bitcast_fusion.1) | copy-start | bytes 3145732
  143.2 3.6 %collective-permute-start.6 = (bf16[64,256]{1,0:T(8,128)(2,1)S(1)}, bf16[64,256]{1,0:T(8,128)(2,1)S(1)}, u32[]{:S(2)}, u32[]{:S(2)}) collective-permute-start(bf16[64,256]{1,0:T(8,128)(2,1)S(1)} %get-tuple-element.5), channel_id=1, source_target_pairs={{0,1},{2,3},{4,5},{6,7},{8,9},{10,11},{12,13},{14,15},{16,17},{18,... | collective-permute-start | bytes 98312 | tf_op jit(solution)/shard_map/ppermute | solution.py:18
  145.3 3.1 %collective-permute-start.7 = (bf16[64,256]{1,0:T(8,128)(2,1)S(1)}, bf16[64,256]{1,0:T(8,128)(2,1)S(1)}, u32[]{:S(2)}, u32[]{:S(2)}) collective-permute-start(bf16[64,256]{1,0:T(8,128)(2,1)S(1)} %get-tuple-element.6), channel_id=1, source_target_pairs={{1,0},{3,2},{5,4},{7,6},{9,8},{11,10},{13,12},{15,14},{17,16},{19,... | collective-permute-start | bytes 98312 | tf_op jit(solution)/shard_map/ppermute | solution.py:21
  151.6 7.7 %copy-start.3 = (f32[32,8,8,128]{3,2,1,0:T(8,128)S(1)}, f32[32,8,8,128]{3,2,1,0:T(8,128)}, u32[]{:S(2)}) copy-start(f32[32,8,8,128]{3,2,1,0:T(8,128)} %copy-done.1) | copy-start | bytes 3145732
  151.6 7.8 %copy-start.5 = (f32[32,8,8,128]{3,2,1,0:T(8,128)S(1)}, f32[32,8,8,128]{3,2,1,0:T(8,128)}, u32[]{:S(2)}) copy-start(f32[32,8,8,128]{3,2,1,0:T(8,128)} %copy-done.4) | copy-start | bytes 3145732
Sparse Core Ops, SparseCore 0:
  10.1 63.0 all-gather.1
